TPU v7x, 512 devices: a whole 4x8x8 slice. The times are simulated.
512 devices in a mesh: rep: 4 (over z_hi), dp: 16 (over y, core), tensor: 8 (over x, z_lo).
Axes of the slice: x: 4, y: 8, z: 8 (z_hi: 4, z_lo: 2; z = z_hi * 2 + z_lo), core: 2. Of those that a mesh axis runs over, the one named last changes fastest.
Arguments:
- grad_proj: float32 [64, 3072, 1536], P(('rep', 'dp'), 'tensor'), as said below
- grad_conv: float32 [64, 4, 3328], P(('rep', 'dp'), None, 'tensor'), may hold values from -24 to 24
- param_proj: float32 [3072, 1536], P('tensor', 'dp'), may hold values from -6 to 6
- m_proj: float32 [3072, 1536], P('tensor', 'dp'), may hold values from -2 to 2
- v_proj: float32 [3072, 1536], P('tensor', 'dp'), may hold values from 0.02 to 0.2
- ema_proj: float32 [3072, 1536], P(('tensor', 'dp')), may hold values from -6 to 6
- param_conv: float32 [4, 3328], P(None, 'tensor'), may hold values from -3 to 3
- m_conv: float32 [4, 3328], P(None, 'tensor'), may hold values from -2 to 2
- v_conv: float32 [4, 3328], P(None, 'tensor'), may hold values from 0.02 to 0.2
Outputs:
- new_param_proj: float32 [3072, 1536], P('tensor', 'dp')
- new_m_proj: float32 [3072, 1536], P('tensor', 'dp')
- new_v_proj: float32 [3072, 1536], P('tensor', 'dp')
- new_ema_proj: float32 [3072, 1536], P(('tensor', 'dp'))
- weights_proj: bfloat16 [3072, 1536], P('tensor')
- new_param_conv: float32 [4, 3328], P(None, 'tensor')
- new_m_conv: float32 [4, 3328], P(None, 'tensor')
- new_v_conv: float32 [4, 3328], P(None, 'tensor')
Inputs may be any that keep to these rules, and one draw needn't show every extreme that they name: `grad_proj`: Real-valued gradients with entries of magnitude below 3100.
All inputs are finite; a program needn't handle non-finite values.
Results may differ from a plain program's by a relative error of at most 0.001.
Values may be sent and summed in bfloat16 or wider, within the bound.
A program may use at most 64 MiB of HBM per device.

v0:
```python
import math
import jax
import jax.numpy as jnp
from jax import lax
from jax.sharding import PartitionSpec as P

D = 1536
INNER = 3072
CONV = 3328
KCONV = 4


def adamw_step(param_in, first_in, second_in, grad_in):
    first_out = 0.9 * first_in + 0.1 * grad_in
    second_out = 0.95 * second_in + 0.05 * grad_in * grad_in
    bias_one = 1.0 - 0.9**10
    bias_two = 1.0 - 0.95**10
    update = first_out / bias_one / (jnp.sqrt(second_out / bias_two) + 1e-08)
    param_out = param_in - 0.25 * (update + 0.1 * param_in)
    return (param_out, first_out, second_out)


def clip_from(square_sum):
    clip_limit = 0.5 * math.sqrt(INNER * D + KCONV * CONV)
    return jnp.minimum(1.0, clip_limit / (jnp.sqrt(square_sum) + 1e-06))


def body(grad_proj, grad_conv, param_proj, m_proj, v_proj, ema_proj, param_conv, m_conv, v_conv):
    replica_count = lax.axis_size("rep") * lax.axis_size("dp")
    conv_avg = lax.psum(grad_conv[0], ("rep", "dp")) / replica_count
    conv_square = jnp.sum(conv_avg * conv_avg)
    first_owner = lax.axis_index("dp") == 0
    owner_sum = lax.psum_scatter(grad_proj[0], "dp", scatter_dimension=1, tiled=True)
    proj_avg = lax.psum(owner_sum, "rep") / replica_count
    conv_share = jnp.where(first_owner, conv_square, jnp.float32(0.0))
    square_sum = lax.psum(jnp.sum(proj_avg * proj_avg) + conv_share, ("dp", "tensor"))
    clip_factor = clip_from(square_sum)
    new_param_proj, new_m_proj, new_v_proj = adamw_step(
        param_proj, m_proj, v_proj, clip_factor * proj_avg
    )
    new_param_conv, new_m_conv, new_v_conv = adamw_step(
        param_conv, m_conv, v_conv, clip_factor * conv_avg
    )
    ema_count = ema_proj.shape[0]
    full_block = lax.all_gather(
        new_param_proj.astype(jnp.bfloat16), "dp", axis=1, tiled=True
    ).astype(new_param_proj.dtype)
    weights_proj = full_block.astype(jnp.bfloat16)
    row_block = lax.dynamic_slice_in_dim(full_block, lax.axis_index("dp") * ema_count, ema_count, 0)
    new_ema_proj = 0.9 * ema_proj + 0.1 * row_block
    return (
        new_param_proj,
        new_m_proj,
        new_v_proj,
        new_ema_proj,
        weights_proj,
        new_param_conv,
        new_m_conv,
        new_v_conv,
    )


def solution(mesh):
    in_specs = (
        P(("rep", "dp"), "tensor", None),
        P(("rep", "dp"), None, "tensor"),
        P("tensor", "dp"),
        P("tensor", "dp"),
        P("tensor", "dp"),
        P(("tensor", "dp"), None),
        P(None, "tensor"),
        P(None, "tensor"),
        P(None, "tensor"),
    )
    out_specs = (
        P("tensor", "dp"),
        P("tensor", "dp"),
        P("tensor", "dp"),
        P(("tensor", "dp"), None),
        P("tensor", None),
        P(None, "tensor"),
        P(None, "tensor"),
        P(None, "tensor"),
    )
    return jax.shard_map(body, mesh=mesh, in_specs=in_specs, out_specs=out_specs, check_vma=False)
```

profile of v0, /device:TPU:1, one launch (start us, length us, event | category | flops | bytes accessed | tf_op | source)
XLA Modules:
  0.0 549.1 jit_solution(13845586338401462347)
XLA Ops:
  7.2 0.0 reduce-scatter.2.cloned.1.call-start
  7.2 3.1 copy.19
  10.3 0.0 copy-start.8
  10.3 0.0 copy-start.2
  10.3 0.0 copy-start.3
  10.3 0.0 copy-start.4
  10.3 0.0 reduce-scatter.2.cloned.1.call-update
  10.3 0.0 copy-start.1
  10.3 0.0 all-reduce.2.cloned.1.call-start
  10.4 66.1 %reduce-scatter.2.cloned.1.call-done = f32[384,96]{0,1:T(8,128)} async-done(((f32[384,1536]{0,1:T(8,128)}), f32[384,96]{0,1:T(8,128)}) %reduce-scatter.2.cloned.1.call-update) | async-done | bytes 147472 | tf_op jit(solution)/shard_map/reduce_scatter | solution.py:33
  76.5 0.0 all-reduce.2.cloned.1.call-update
  76.5 0.0 copy-start.5
  76.5 0.0 copy-start.6
  76.5 0.0 copy-start.7
  76.5 0.0 all-gather.2.cloned.1.call-start
  76.6 0.0 copy-done.8
  76.6 142.5 %psum.22 = f32[4,416]{1,0:T(4,128)S(1)} all-reduce(f32[4,416]{1,0:T(4,128)S(1)} %bitcast.3), channel_id=1, replica_groups=mesh['rep'=4,'dp'=16,'tensor'=8] {'rep','dp'}, use_global_device_ids=true, to_apply=%region_3.0 | all-reduce | flops 1664 | bytes 13312 | tf_op jit(solution)/shard_map/psum | solution.py:30
  219.1 0.6 multiply_reduce_fusion.1
  220.3 0.0 all-reduce.2.cloned.1.call-done
  220.4 1.6 multiply_reduce_fusion
  222.6 270.7 %psum.23 = f32[]{:T(128)} all-reduce(f32[]{:T(128)S(6)} %add.50), channel_id=1, replica_groups=mesh['rep'=4,'dp'=16,'tensor'=8] {'dp','tensor'}, use_global_device_ids=true, to_apply=%region_5.6 | all-reduce | flops 1 | bytes 8 | tf_op jit(solution)/shard_map/psum | solution.py:36
  494.0 0.0 copy-done.2
  494.0 0.0 copy-done.3
  494.0 0.0 copy-done.4
  494.0 1.8 fusion.3
  495.7 0.0 all-gather.2.cloned.1.call-update
  495.8 0.0 copy-done.1
  495.8 0.3 copy.20
  496.1 0.0 copy-done.5
  496.1 0.0 copy-done.6
  496.1 0.0 copy-done.7
  496.1 0.6 multiply_subtract_fusion.1
  496.7 42.1 %all-gather.2.cloned.1.call-done = bf16[384,1536]{0,1:T(8,128)(2,1)} async-done(((bf16[384,96]{0,1:T(8,128)(2,1)}), bf16[384,1536]{0,1:T(8,128)(2,1)}) %all-gather.2.cloned.1.call-update) | async-done | bytes 1179664 | tf_op jit(solution)/shard_map/all_gather | solution.py:45
  538.8 0.0 copy-start
  538.8 1.4 multiply_add_fusion
  540.3 0.9 copy.21
  541.2 0.0 copy-done
  541.2 1.4 copy.22
Async XLA Ops:
  7.2 69.3 %reduce-scatter.2.cloned.1.call-start = ((), (), s32[]{:S(2)}) async-start(), calls=%async_computation.1 | async-start | bytes 2506752 | tf_op jit(solution)/shard_map/reduce_scatter | solution.py:33
  10.3 66.3 %copy-start.8 = (f32[1,4,416]{2,1,0:T(4,128)S(1)}, f32[1,4,416]{2,1,0:T(4,128)}, u32[]{:S(2)}) copy-start(f32[1,4,416]{2,1,0:T(4,128)} %param.10) | copy-start | bytes 19972
  10.3 483.7 %copy-start.2 = (f32[384,96]{0,1:T(8,128)S(1)}, f32[384,96]{0,1:T(8,128)}, u32[]{:S(2)}) copy-start(f32[384,96]{0,1:T(8,128)} %param.11) | copy-start | bytes 442372
  10.3 483.7 %copy-start.3 = (f32[384,96]{0,1:T(8,128)S(1)}, f32[384,96]{0,1:T(8,128)}, u32[]{:S(2)}) copy-start(f32[384,96]{0,1:T(8,128)} %param.12) | copy-start | bytes 442372
  10.3 483.7 %copy-start.4 = (f32[384,96]{0,1:T(8,128)S(1)}, f32[384,96]{0,1:T(8,128)}, u32[]{:S(2)}) copy-start(f32[384,96]{0,1:T(8,128)} %param.13) | copy-start | bytes 442372
  10.3 485.4 %copy-start.1 = (f32[24,1536]{1,0:T(8,128)S(1)}, f32[24,1536]{1,0:T(8,128)}, u32[]{:S(2)}) copy-start(f32[24,1536]{1,0:T(8,128)} %param.14) | copy-start | bytes 442372
  10.3 210.0 %all-reduce.2.cloned.1.call-start = ((), (), s32[]{:S(2)}) async-start(), calls=%async_computation.2 | async-start | bytes 294912 | tf_op jit(solution)/shard_map/psum | solution.py:34
  76.5 419.6 %copy-start.5 = (f32[4,416]{1,0:T(4,128)S(1)}, f32[4,416]{1,0:T(4,128)}, u32[]{:S(2)}) copy-start(f32[4,416]{1,0:T(4,128)} %param.15) | copy-start | bytes 19972
  76.5 419.5 %copy-start.6 = (f32[4,416]{1,0:T(4,128)S(1)}, f32[4,416]{1,0:T(4,128)}, u32[]{:S(2)}) copy-start(f32[4,416]{1,0:T(4,128)} %param.16) | copy-start | bytes 19972
  76.5 419.5 %copy-start.7 = (f32[4,416]{1,0:T(4,128)S(1)}, f32[4,416]{1,0:T(4,128)}, u32[]{:S(2)}) copy-start(f32[4,416]{1,0:T(4,128)} %param.17) | copy-start | bytes 19972
  76.5 462.3 %all-gather.2.cloned.1.call-start = ((), (), s32[]{:S(2)}) async-start(), calls=%async_computation.3 | async-start | bytes 1253376 | tf_op jit(solution)/shard_map/all_gather | solution.py:45
  538.8 2.3 copy-start
Sparse Core Ops, SparseCore 0:
  10.8 65.6 reduce-scatter.1
  79.4 55.1 all-reduce.1
  495.9 42.8 all-gather.1
where the time goes:
time: 549 us
  blocking collectives  413 us (75%)
  waiting for transfers between devices  108 us (20%)
  between operations  15.9 us (3%)
  other arithmetic  5.98 us (1%)
  local copies, waits for them, and re-layouts  5.74 us (1%)
    psum x1, blocking collectives, body(): lax.psum(jnp.sum(proj_avg * proj_avg) + conv_share, ('dp', 'tensor'))  271 us
    psum x1, blocking collectives, body(): conv_avg = lax.psum(grad_conv[0], ('rep', 'dp')) / replica_count  142 us
    reduce_scatter x1, waiting for transfers between devices, body(): lax.psum_scatter(grad_proj[0], 'dp', scatter_dimension=1, tiled=True)  66.1 us
    all_gather x1, waiting for transfers between devices, body(): lax.all_gather(new_param_proj.astype(jnp.bfloat16), 'dp', axis=1, tiled=T...  42.1 us
  transfers between devices with their start and end apart: 3, of which 2 were waited for; matrix products, arithmetic and copies ran while one was open for 0% of the time, Pallas kernels for 0%

commit v1 on v0

--- a/solution.py
+++ b/solution.py
@@ -27,7 +27,7 @@
 
 def body(grad_proj, grad_conv, param_proj, m_proj, v_proj, ema_proj, param_conv, m_conv, v_conv):
     replica_count = lax.axis_size("rep") * lax.axis_size("dp")
-    conv_avg = lax.psum(grad_conv[0], ("rep", "dp")) / replica_count
+    conv_avg = lax.psum(lax.psum(grad_conv[0], "rep"), "dp") / replica_count
     conv_square = jnp.sum(conv_avg * conv_avg)
     first_owner = lax.axis_index("dp") == 0
     owner_sum = lax.psum_scatter(grad_proj[0], "dp", scatter_dimension=1, tiled=True)

time: 549 us -> 466 us (0.85)
  blocking collectives: 413 us -> 309 us
  waiting for transfers between devices: 108 us -> 129 us
    psum x1 -> x2, blocking collectives: 142 us -> 39.7 us  [body(): conv_avg = lax.psum(lax.psum(grad_conv[0], 'rep'), 'dp') / replica_count]
    psum x1, waiting for transfers between devices: 0.02 us -> 16.9 us  [body(): proj_avg = lax.psum(owner_sum, 'rep') / replica_count]
  transfers between devices with their start and end apart: 3 -> 3, of which waited for: 2 -> 3; matrix products, arithmetic and copies ran while one was open for 0% -> 0% of each run, Pallas kernels for 0% -> 0%
where the time goes in v1:
time: 466 us
  blocking collectives  309 us (66%)
  waiting for transfers between devices  129 us (28%)
  between operations  15.9 us (3%)
  other arithmetic  5.98 us (1%)
  local copies, waits for them, and re-layouts  5.73 us (1%)
    psum x1, blocking collectives, body(): lax.psum(jnp.sum(proj_avg * proj_avg) + conv_share, ('dp', 'tensor'))  270 us
    reduce_scatter x1, waiting for transfers between devices, body(): lax.psum_scatter(grad_proj[0], 'dp', scatter_dimension=1, tiled=True)  66.1 us
    all_gather x1, waiting for transfers between devices, body(): lax.all_gather(new_param_proj.astype(jnp.bfloat16), 'dp', axis=1, tiled=T...  45.7 us
    psum x2, blocking collectives, body(): conv_avg = lax.psum(lax.psum(grad_conv[0], 'rep'), 'dp') / replica_count  39.7 us
    psum x1, waiting for transfers between devices, body(): proj_avg = lax.psum(owner_sum, 'rep') / replica_count  16.9 us
  transfers between devices with their start and end apart: 3, of which 3 were waited for; matrix products, arithmetic and copies ran while one was open for 0% of the time, Pallas kernels for 0%

profile of v1, /device:TPU:1, one launch (start us, length us, event | category | flops | bytes accessed | tf_op | source)
XLA Modules:
  0.0 465.9 jit_solution(9265639887636503686)
XLA Ops:
  7.2 0.0 reduce-scatter.2.cloned.1.call-start
  7.2 3.1 copy.19
  10.3 0.0 copy-start.8
  10.3 0.0 copy-start.2
  10.3 0.0 copy-start.3
  10.3 0.0 copy-start.4
  10.3 0.0 reduce-scatter.2.cloned.1.call-update
  10.3 0.0 copy-start.1
  10.3 0.0 all-reduce.2.cloned.1.call-start
  10.4 66.1 %reduce-scatter.2.cloned.1.call-done = f32[384,96]{0,1:T(8,128)} async-done(((f32[384,1536]{0,1:T(8,128)}), f32[384,96]{0,1:T(8,128)}) %reduce-scatter.2.cloned.1.call-update) | async-done | bytes 147472 | tf_op jit(solution)/shard_map/reduce_scatter | solution.py:33
  76.5 0.0 all-reduce.2.cloned.1.call-update
  76.5 0.0 copy-start.5
  76.5 0.0 copy-start.6
  76.5 0.0 copy-start.7
  76.5 0.0 all-gather.2.cloned.1.call-start
  76.6 0.0 copy-done.8
  76.6 10.4 %psum.29 = f32[4,416]{1,0:T(4,128)S(1)} all-reduce(f32[4,416]{1,0:T(4,128)S(1)} %bitcast.3), channel_id=1, replica_groups=mesh['rep'=4,'dp'=16,'tensor'=8] {'rep'}, use_global_device_ids=true, to_apply=%region_3.0 | all-reduce | flops 1664 | bytes 13312 | tf_op jit(solution)/shard_map/psum | solution.py:30
  87.0 29.3 %psum.30 = f32[4,416]{1,0:T(4,128)S(1)} all-reduce(f32[4,416]{1,0:T(4,128)S(1)} %psum.29), channel_id=1, replica_groups=mesh['rep'=4,'dp'=16,'tensor'=8] {'dp'}, use_global_device_ids=true, to_apply=%region_4.0 | all-reduce | flops 1664 | bytes 13312 | tf_op jit(solution)/shard_map/psum | solution.py:30
  116.3 0.6 multiply_reduce_fusion.1
  117.5 16.9 %all-reduce.2.cloned.1.call-done = f32[384,96]{0,1:T(8,128)} async-done(((f32[384,96]{0,1:T(8,128)}), f32[384,96]{0,1:T(8,128)}) %all-reduce.2.cloned.1.call-update) | async-done | bytes 147472 | tf_op jit(solution)/shard_map/psum | solution.py:34
  134.4 1.6 multiply_reduce_fusion
  136.6 269.8 %psum.31 = f32[]{:T(128)} all-reduce(f32[]{:T(128)S(6)} %add.52), channel_id=1, replica_groups=mesh['rep'=4,'dp'=16,'tensor'=8] {'dp','tensor'}, use_global_device_ids=true, to_apply=%region_6.7 | all-reduce | flops 1 | bytes 8 | tf_op jit(solution)/shard_map/psum | solution.py:36
  407.1 0.0 copy-done.2
  407.1 0.0 copy-done.3
  407.1 0.0 copy-done.4
  407.2 1.8 fusion.3
  408.9 0.0 all-gather.2.cloned.1.call-update
  408.9 0.0 copy-done.1
  409.0 0.3 copy.20
  409.2 0.0 copy-done.5
  409.2 0.0 copy-done.6
  409.2 0.0 copy-done.7
  409.3 0.6 multiply_subtract_fusion.1
  409.9 45.7 %all-gather.2.cloned.1.call-done = bf16[384,1536]{0,1:T(8,128)(2,1)} async-done(((bf16[384,96]{0,1:T(8,128)(2,1)}), bf16[384,1536]{0,1:T(8,128)(2,1)}) %all-gather.2.cloned.1.call-update) | async-done | bytes 1179664 | tf_op jit(solution)/shard_map/all_gather | solution.py:45
  455.6 0.0 copy-start
  455.6 1.4 multiply_add_fusion
  457.0 0.9 copy.21
  457.9 0.0 copy-done
  457.9 1.4 copy.22
Async XLA Ops:
  7.2 69.3 %reduce-scatter.2.cloned.1.call-start = ((), (), s32[]{:S(2)}) async-start(), calls=%async_computation.1 | async-start | bytes 2506752 | tf_op jit(solution)/shard_map/reduce_scatter | solution.py:33
  10.3 66.3 %copy-start.8 = (f32[1,4,416]{2,1,0:T(4,128)S(1)}, f32[1,4,416]{2,1,0:T(4,128)}, u32[]{:S(2)}) copy-start(f32[1,4,416]{2,1,0:T(4,128)} %param.10) | copy-start | bytes 19972
  10.3 396.8 %copy-start.2 = (f32[384,96]{0,1:T(8,128)S(1)}, f32[384,96]{0,1:T(8,128)}, u32[]{:S(2)}) copy-start(f32[384,96]{0,1:T(8,128)} %param.11) | copy-start | bytes 442372
  10.3 396.8 %copy-start.3 = (f32[384,96]{0,1:T(8,128)S(1)}, f32[384,96]{0,1:T(8,128)}, u32[]{:S(2)}) copy-start(f32[384,96]{0,1:T(8,128)} %param.12) | copy-start | bytes 442372
  10.3 396.8 %copy-start.4 = (f32[384,96]{0,1:T(8,128)S(1)}, f32[384,96]{0,1:T(8,128)}, u32[]{:S(2)}) copy-start(f32[384,96]{0,1:T(8,128)} %param.13) | copy-start | bytes 442372
  10.3 398.6 %copy-start.1 = (f32[24,1536]{1,0:T(8,128)S(1)}, f32[24,1536]{1,0:T(8,128)}, u32[]{:S(2)}) copy-start(f32[24,1536]{1,0:T(8,128)} %param.14) | copy-start | bytes 442372
  10.3 124.1 %all-reduce.2.cloned.1.call-start = ((), (), s32[]{:S(2)}) async-start(), calls=%async_computation.2 | async-start | bytes 294912 | tf_op jit(solution)/shard_map/psum | solution.py:34
  76.5 332.7 %copy-start.5 = (f32[4,416]{1,0:T(4,128)S(1)}, f32[4,416]{1,0:T(4,128)}, u32[]{:S(2)}) copy-start(f32[4,416]{1,0:T(4,128)} %param.15) | copy-start | bytes 19972
  76.5 332.7 %copy-start.6 = (f32[4,416]{1,0:T(4,128)S(1)}, f32[4,416]{1,0:T(4,128)}, u32[]{:S(2)}) copy-start(f32[4,416]{1,0:T(4,128)} %param.16) | copy-start | bytes 19972
  76.5 332.7 %copy-start.7 = (f32[4,416]{1,0:T(4,128)S(1)}, f32[4,416]{1,0:T(4,128)}, u32[]{:S(2)}) copy-start(f32[4,416]{1,0:T(4,128)} %param.17) | copy-start | bytes 19972
  76.5 379.1 %all-gather.2.cloned.1.call-start = ((), (), s32[]{:S(2)}) async-start(), calls=%async_computation.3 | async-start | bytes 1253376 | tf_op jit(solution)/shard_map/all_gather | solution.py:45
  455.6 2.3 copy-start
Sparse Core Ops, SparseCore 0:
  10.8 65.6 reduce-scatter.1
  79.4 54.9 all-reduce.1
  409.1 46.4 all-gather.1
